TPU v7x, 32 devices: a whole 2x2x4 slice. The times are simulated.
32 devices in a mesh: pb: 4 (over y, core), ka: 8 (over z, x).
Axes of the slice: x: 2, y: 2, z: 4, core: 2. Of those that a mesh axis runs over, the one named last changes fastest.
Arguments:
- queries: float32 [2048, 128], P('pb'), may hold values from -36 to 36
- cache_keys: float32 [65536, 128], P('ka'), may hold values from -4 to 4
- cache_values: float32 [65536, 128], P('ka'), may hold values from -6 to 6
- kept_index: int32 [4096], P('ka'), may hold values from 0 to 65535, as said below
Outputs:
- fitted: float32 [4096, 128], P('ka')
Inputs may be any that keep to these rules, and one draw needn't show every extreme that they name: `kept_index`: Increasing; the t-th kept index lies among the cache rows t * (16) to (t + 1) * 16 - 1, so the kept keys of a device are rows of its own block of the cache.
All inputs are finite; a program needn't handle non-finite values.
Results may differ from a plain program's by a relative error of at most 0.0003.
Values sent between devices are 32-bit elements; how exact they have to be, the bound alone decides.
A program may use at most 128 MiB of HBM per device.

v0:
```python
import math
import jax
import jax.numpy as jnp
from jax import lax
from jax.sharding import PartitionSpec as P

ITERS = 2
ridge_weight = 0.01
highest = lax.Precision.HIGHEST


def merged_2(part, axis, combine):
    gathered = jax.tree.map(lambda a: lax.all_gather(a, axis), part)

    def take(source):
        return jax.tree.map(lambda a: lax.dynamic_index_in_dim(a, source, 0, False), gathered)

    return lax.fori_loop(
        1, lax.axis_size(axis), lambda source, state: combine(state, take(source)), take(0)
    )


def contract_rows(left_side, right_side):
    return lax.dot_general(
        left_side,
        right_side,
        (((0,), (0,)), ((), ())),
        precision=highest,
        preferred_element_type=jnp.float32,
    )


def contract_cols(left_side, right_side):
    return lax.dot_general(
        left_side,
        right_side,
        (((1,), (1,)), ((), ())),
        precision=highest,
        preferred_element_type=jnp.float32,
    )


def joint_scale(top_one, total_one, top_two, total_two):
    top_joint = jnp.maximum(top_one, top_two)
    factor_one = jnp.exp(top_one - top_joint)
    factor_two = jnp.exp(top_two - top_joint)
    return (top_joint, total_one * factor_one + total_two * factor_two, factor_one, factor_two)


def combine_target(part_one, part_two):
    top_joint, total_sum, factor_one, factor_two = joint_scale(
        part_one[0], part_one[1], part_two[0], part_two[1]
    )
    numerator = part_one[2] * factor_one[:, None] + part_two[2] * factor_two[:, None]
    return (top_joint, total_sum, numerator)


def combine_stats(part_one, part_two):
    target_part = combine_target(part_one[0:3], part_two[0:3])
    kept_top, kept_total, factor_one, factor_two = joint_scale(
        part_one[3], part_one[4], part_two[3], part_two[4]
    )
    return target_part + (kept_top, kept_total)


def key_rows(weights, updates):
    return lax.psum(contract_rows(weights, updates), "pb")


def forward_terms(weights, direction):
    return (
        jnp.dot(weights, direction, precision=highest, preferred_element_type=jnp.float32),
        jnp.sum(direction * direction, axis=0),
    )


def residual_total(column_part):
    return lax.psum(column_part, "ka")


def direction_total(column_part):
    return lax.psum(column_part, "ka")


def shards(queries, cache_keys, cache_values, kept_index):
    head_width = queries.shape[1]
    inverse_root = 1.0 / math.sqrt(head_width)
    cache_rows = cache_keys.shape[0]
    block_size = min(1024, cache_rows)
    target_stats = None
    for block_number in range(cache_rows // block_size):
        keys_block = lax.slice_in_dim(
            cache_keys, block_number * block_size, (block_number + 1) * block_size, axis=0
        )
        values_block = lax.slice_in_dim(
            cache_values, block_number * block_size, (block_number + 1) * block_size, axis=0
        )
        scores = contract_cols(queries, keys_block) * inverse_root
        top_block = jnp.max(scores, axis=1)
        exponent_block = jnp.exp(scores - top_block[:, None])
        stats_block = (
            top_block,
            jnp.sum(exponent_block, axis=1),
            jnp.dot(
                exponent_block, values_block, precision=highest, preferred_element_type=jnp.float32
            ),
        )
        target_stats = (
            stats_block if target_stats is None else combine_target(target_stats, stats_block)
        )
    local_kept = kept_index - lax.axis_index("ka") * cache_rows
    kept_keys = jnp.take(cache_keys, local_kept, axis=0)
    kept_scores = contract_cols(queries, kept_keys) * inverse_root
    kept_top = jnp.max(kept_scores, axis=1)
    kept_exponent = jnp.exp(kept_scores - kept_top[:, None])
    merged = merged_2(
        (
            target_stats[0],
            target_stats[1],
            target_stats[2],
            kept_top,
            jnp.sum(kept_exponent, axis=1),
        ),
        "ka",
        combine_stats,
    )
    target = merged[2] / merged[1][:, None]
    weights = kept_exponent * (jnp.exp(kept_top - merged[3]) / merged[4])[:, None]
    residual = key_rows(weights, target)
    fitted = jnp.zeros_like(residual)
    direction = residual
    norm_now = residual_total(jnp.sum(residual * residual, axis=0))
    for iteration in range(ITERS):
        final_turn = iteration + 1 == ITERS
        update_part, square_part = forward_terms(weights, direction)
        updates = lax.psum(update_part, "ka")
        operator_image = key_rows(weights, updates) + ridge_weight * direction
        step_length = norm_now / direction_total(jnp.sum(direction * operator_image, axis=0))
        fitted = fitted + step_length * direction
        if not final_turn:
            residual = residual - step_length * operator_image
            norm_next = residual_total(jnp.sum(residual * residual, axis=0))
            direction = residual + norm_next / norm_now * direction
            norm_now = norm_next
    return fitted


def solution(mesh):
    in_specs = (P("pb", None), P("ka", None), P("ka", None), P("ka"))
    out_specs = P("ka", None)
    return jax.shard_map(shards, mesh=mesh, in_specs=in_specs, out_specs=out_specs, check_vma=False)
```

profile of v0, /device:TPU:0, one launch (start us, length us, event | category | flops | bytes accessed | tf_op | source)
XLA Modules:
  0.0 488.6 jit_solution(1318856065512095628)
XLA Ops:
  7.5 3.1 multiply_reduce_fusion
  10.6 3.0 multiply_reduce_fusion.1
  13.7 2.0 multiply_reduce_fusion.2
  15.6 2.0 multiply_reduce_fusion.3
  17.6 2.0 multiply_reduce_fusion.4
  19.6 2.0 multiply_reduce_fusion.5
  21.6 2.4 multiply_reduce_fusion.6
  24.0 2.0 multiply_reduce_fusion.7
  26.1 2.0 fusion.18
  28.1 2.0 fusion.19
  30.1 2.0 fusion.20
  32.1 2.0 fusion.21
  34.1 2.2 fusion.22
  36.3 2.0 fusion.23
  38.4 2.1 fusion.36
  40.5 2.7 fusion.37
  43.8 1.1 copy-done.2
  50.7 28.0 %all-gather.3 = f32[8,1,512]{2,1,0:T(1,128)S(1)} all-gather(f32[1,1,512]{2,1,0:T(1,128)S(1)} %get-tuple-element.319), channel_id=1, replica_groups=mesh['pb'=4,'ka'=8] {'ka'}, dimensions={0}, use_global_device_ids=true | all-gather | bytes 18432 | tf_op jit(solution)/shard_map/all_gather | solution.py:13
  78.7 26.2 %all-gather.4 = f32[8,1,512]{2,1,0:T(1,128)S(1)} all-gather(f32[1,1,512]{2,1,0:T(1,128)S(1)} %get-tuple-element.318), channel_id=1, replica_groups=mesh['pb'=4,'ka'=8] {'ka'}, dimensions={0}, use_global_device_ids=true | all-gather | bytes 18432 | tf_op jit(solution)/shard_map/all_gather | solution.py:13
  105.0 3.2 gather_fusion
  108.2 1.1 fusion.106
  109.2 26.0 %all-gather.5 = f32[8,1,512]{2,1,0:T(1,128)S(1)} all-gather(f32[1,1,512]{2,1,0:T(1,128)S(1)} %bitcast.74), channel_id=3, replica_groups=mesh['pb'=4,'ka'=8] {'ka'}, dimensions={0}, use_global_device_ids=true | all-gather | bytes 18432 | tf_op jit(solution)/shard_map/all_gather | solution.py:13
  135.5 26.0 %all-gather.6 = f32[8,1,512]{2,1,0:T(1,128)S(1)} all-gather(f32[1,1,512]{2,1,0:T(1,128)S(1)} %bitcast.91), channel_id=4, replica_groups=mesh['pb'=4,'ka'=8] {'ka'}, dimensions={0}, use_global_device_ids=true | all-gather | bytes 18432 | tf_op jit(solution)/shard_map/all_gather | solution.py:13
  161.5 1.0 slice.80
  162.4 9.3 %while.23 = (s32[]{:T(128)}, f32[512]{0:T(512)S(1)}, f32[512]{0:T(512)S(1)}, f32[512,128]{1,0:T(8,128)S(1)}, f32[512]{0:T(512)S(1)}, /*index=5*/f32[512]{0:T(512...) while((s32[]{:T(128)}, f32[512]{0:T(512)S(1)}, ...), condition=%wide.region_19.20_spmd, body=%wide.region_18.19_spmd.sunk | while | flops 202757 | bytes 835779 | solution.py:18
  162.5 1.2 fusion.120
  163.9 1.2 fusion.120
  165.2 1.2 fusion.120
  166.5 1.2 fusion.120
  167.8 1.2 fusion.120
  169.2 1.2 fusion.120
  170.5 1.2 fusion.120
  171.7 1.8 fusion.88
  173.6 29.4 %all-reduce.7.cloned.1.call-done = f32[512,128]{1,0:T(8,128)} async-done(((f32[512,128]{1,0:T(8,128)}), f32[512,128]{1,0:T(8,128)}) %all-reduce.7.cloned.1.call-update) | async-done | bytes 262160 | tf_op jit(solution)/shard_map/psum | solution.py:67
  203.0 3.5 fusion.86
  206.6 70.7 %all-reduce.9.cloned.1.call-done = f32[512,128]{1,0:T(8,128)} async-done(((f32[512,128]{1,0:T(8,128)}), f32[512,128]{1,0:T(8,128)}) %all-reduce.9.cloned.1.call-update) | async-done | bytes 262160 | tf_op jit(solution)/shard_map/psum | solution.py:136
  277.2 2.7 fusion.84
  280.0 31.4 %all-reduce.11.cloned.1.call-done = f32[512,128]{1,0:T(8,128)} async-done(((f32[512,128]{1,0:T(8,128)}), f32[512,128]{1,0:T(8,128)}) %all-reduce.11.cloned.1.call-update) | async-done | bytes 262160 | tf_op jit(solution)/shard_map/psum | solution.py:67
  311.4 1.0 multiply_reduce_fusion.10
  312.4 21.3 %all-reduce = (f32[128]{0:T(128)S(1)}, f32[128]{0:T(128)S(1)}) all-reduce(f32[128]{0:T(128)S(1)} %get-tuple-element.277, f32[128]{0:T(128)S(1)} %get-tuple-element.276), channel_id=1, replica_groups=mesh['pb'=4,'ka'=8] {'ka'}, use_global_device_ids=true, to_apply=%region_22.23 | all-reduce | flops 256 | bytes 2048 | tf_op jit(solution)/shard_map/psum | solution.py:78
  333.8 1.0 multiply_reduce_fusion.9
  334.8 17.3 %psum.68 = f32[128]{0:T(128)S(1)} all-reduce(f32[128]{0:T(128)S(1)} %multiply_reduce_fusion.9), channel_id=1, replica_groups=mesh['pb'=4,'ka'=8] {'ka'}, use_global_device_ids=true, to_apply=%region_28.29 | all-reduce | flops 128 | bytes 1024 | tf_op jit(solution)/shard_map/psum | solution.py:78
  352.1 3.5 fusion.82
  355.7 68.5 %all-reduce.13.cloned.1.call-done = f32[512,128]{1,0:T(8,128)} async-done(((f32[512,128]{1,0:T(8,128)}), f32[512,128]{1,0:T(8,128)}) %all-reduce.13.cloned.1.call-update) | async-done | bytes 262160 | tf_op jit(solution)/shard_map/psum | solution.py:136
  424.1 2.7 fusion.80
  426.9 31.4 %all-reduce.15.cloned.1.call-done = f32[512,128]{1,0:T(8,128)} async-done(((f32[512,128]{1,0:T(8,128)}), f32[512,128]{1,0:T(8,128)}) %all-reduce.15.cloned.1.call-update) | async-done | bytes 262160 | tf_op jit(solution)/shard_map/psum | solution.py:67
  458.3 1.1 multiply_reduce_fusion.8
  459.3 21.3 %psum.71 = f32[128]{0:T(128)S(1)} all-reduce(f32[128]{0:T(128)S(1)} %multiply_reduce_fusion.8), channel_id=1, replica_groups=mesh['pb'=4,'ka'=8] {'ka'}, use_global_device_ids=true, to_apply=%region_32.33 | all-reduce | flops 128 | bytes 1024 | tf_op jit(solution)/shard_map/psum | solution.py:82
  (114 shorter events, 9.1 us)
Async XLA Ops:
  6.5 1.0 copy-start
  6.5 154.9 %all-gather.9.cloned.1.call-start = ((), (), s32[]{:S(2)}) async-start(), calls=%async_computation.5 | async-start | bytes 2359296 | tf_op jit(solution)/shard_map/all_gather | solution.py:13
  7.5 6.2 %copy-start.15 = (f32[8192,128]{1,0:T(8,128)S(1)}, f32[8192,128]{1,0:T(8,128)}, u32[]{:S(2)}) copy-start(f32[8192,128]{1,0:T(8,128)} %param.7) | copy-start | bytes 12582916
  13.7 12.4 %copy-start.1 = (f32[512,1024]{1,0:T(8,128)}, f32[512,1024]{1,0:T(8,128)S(1)}, u32[]{:S(2)}) copy-start(f32[512,1024]{1,0:T(8,128)S(1)} %get-tuple-element.346) | copy-start | bytes 6291460
  15.6 12.4 %copy-start.3 = (f32[512,1024]{1,0:T(8,128)}, f32[512,1024]{1,0:T(8,128)S(1)}, u32[]{:S(2)}) copy-start(f32[512,1024]{1,0:T(8,128)S(1)} %get-tuple-element.348) | copy-start | bytes 6291460
  17.6 12.5 %copy-start.5 = (f32[512,1024]{1,0:T(8,128)}, f32[512,1024]{1,0:T(8,128)S(1)}, u32[]{:S(2)}) copy-start(f32[512,1024]{1,0:T(8,128)S(1)} %get-tuple-element.350) | copy-start | bytes 6291460
  19.6 12.5 %copy-start.7 = (f32[512,1024]{1,0:T(8,128)}, f32[512,1024]{1,0:T(8,128)S(1)}, u32[]{:S(2)}) copy-start(f32[512,1024]{1,0:T(8,128)S(1)} %get-tuple-element.352) | copy-start | bytes 6291460
  21.6 12.6 %copy-start.9 = (f32[512,1024]{1,0:T(8,128)}, f32[512,1024]{1,0:T(8,128)S(1)}, u32[]{:S(2)}) copy-start(f32[512,1024]{1,0:T(8,128)S(1)} %get-tuple-element.354) | copy-start | bytes 6291460
  21.6 4.5 copy-start.18
  24.0 12.3 %copy-start.11 = (f32[512,1024]{1,0:T(8,128)}, f32[512,1024]{1,0:T(8,128)S(1)}, u32[]{:S(2)}) copy-start(f32[512,1024]{1,0:T(8,128)S(1)} %get-tuple-element.356) | copy-start | bytes 6291460
  26.0 12.4 %copy-start.13 = (f32[512,1024]{1,0:T(8,128)}, f32[512,1024]{1,0:T(8,128)S(1)}, u32[]{:S(2)}) copy-start(f32[512,1024]{1,0:T(8,128)S(1)} %get-tuple-element.358) | copy-start | bytes 6291460
  43.2 159.8 %all-reduce.7.cloned.1.call-start = ((), (), s32[]{:S(2)}) async-start(), calls=%async_computation | async-start | bytes 524288 | tf_op jit(solution)/shard_map/psum | solution.py:67
  43.3 1.6 copy-start.2
  43.3 2.2 copy-start.4
  44.9 1.7 copy-start.6
  45.5 1.7 copy-start.8
  46.6 1.7 copy-start.10
  47.2 1.7 copy-start.12
  48.3 1.7 copy-start.14
  48.9 56.0 %copy-start.19 = (s32[512]{0:T(512)S(1)}, s32[512]{0:T(512)}, u32[]{:S(2)}) copy-start(s32[512]{0:T(512)} %param.9) | copy-start | bytes 6148
  173.6 103.7 %all-reduce.9.cloned.1.call-start = ((), (), s32[]{:S(2)}) async-start(), calls=%async_computation.1 | async-start | bytes 524288 | tf_op jit(solution)/shard_map/psum | solution.py:136
  203.0 108.4 %copy-start.16 = (f32[512,128]{1,0:T(8,128)S(1)}, f32[512,128]{1,0:T(8,128)}, u32[]{:S(2)}) copy-start(f32[512,128]{1,0:T(8,128)} %all-reduce.7.cloned.1.call-done) | copy-start | bytes 786436
  206.5 104.8 %all-reduce.11.cloned.1.call-start = ((), (), s32[]{:S(2)}) async-start(), calls=%async_computation.2 | async-start | bytes 524288 | tf_op jit(solution)/shard_map/psum | solution.py:67
  280.0 144.2 %all-reduce.13.cloned.1.call-start = ((), (), s32[]{:S(2)}) async-start(), calls=%async_computation.3 | async-start | bytes 524288 | tf_op jit(solution)/shard_map/psum | solution.py:136
  334.8 123.5 %copy-start.17 = (f32[512,128]{1,0:T(8,128)S(1)}, f32[512,128]{1,0:T(8,128)}, u32[]{:S(2)}) copy-start(f32[512,128]{1,0:T(8,128)} %all-reduce.11.cloned.1.call-done) | copy-start | bytes 786436
  355.6 102.6 %all-reduce.15.cloned.1.call-start = ((), (), s32[]{:S(2)}) async-start(), calls=%async_computation.4 | async-start | bytes 524288 | tf_op jit(solution)/shard_map/psum | solution.py:67
Sparse Core Ops, SparseCore 0:
  43.3 52.1 all-gather.8
  173.7 29.2 all-reduce.6
  206.7 70.5 all-reduce.8
  280.1 31.2 all-reduce.10
  355.8 68.3 all-reduce.12
  427.0 31.2 all-reduce.14
where the time goes:
time: 498 us; the launch traced here: 489 us
  waiting for transfers between devices  231 us (46%)
  blocking collectives  166 us (33%)
  matrix products  50.8 us (10%)
  other arithmetic  17.1 us (3%)
  between operations  14 us (3%)
  local copies, waits for them, and re-layouts  8.61 us (2%)
    psum x2, waiting for transfers between devices, shards(): updates = lax.psum(update_part, 'ka')  139 us
    all_gather x4, blocking collectives, merged_2(): gathered = jax.tree.map(lambda a: lax.all_gather(a, axis), part)  106 us
    psum x3, waiting for transfers between devices, key_rows(): return lax.psum(contract_rows(weights, updates), 'pb')  92.1 us
    psum x2, blocking collectives, residual_total(): return lax.psum(column_part, 'ka')  38.6 us
    psum x1, blocking collectives, direction_total(): return lax.psum(column_part, 'ka')  21.3 us
    dot_general x9, matrix products, contract_cols(): lax.dot_general(left_side, right_side, (((1,), (1,)), ((), ())), precisio...  19.5 us
    dot_general x8, matrix products, shards(): jnp.dot(exponent_block, values_block, precision=highest, preferred_elemen...  17 us
  transfers between devices with their start and end apart: 6, of which 5 were waited for; matrix products, arithmetic and copies ran while one was open for 2% of the time, Pallas kernels for 0%

commit v1 on v0

--- a/solution.py
+++ b/solution.py
@@ -75,7 +75,7 @@
 
 
 def residual_total(column_part):
-    return lax.psum(column_part, "ka")
+    return jnp.sum(lax.all_gather(column_part, "ka"), axis=0)
 
 
 def direction_total(column_part):

time: 498 us -> 514 us (1.032)
  blocking collectives: 166 us -> 183 us
    all_gather x0 -> x2, blocking collectives: none -> 38.7 us  [residual_total(): return jnp.sum(lax.all_gather(column_part, 'ka'), axis=0)]
    psum x2 -> x0, blocking collectives: 38.6 us -> none  [residual_total(): return lax.psum(column_part, 'ka')]
    psum x1 -> x2, blocking collectives: 21.3 us -> 38.5 us  [direction_total(): return lax.psum(column_part, 'ka')]
where the time goes in v1:
time: 514 us; the launch traced here: 504 us
  waiting for transfers between devices  230 us (45%)
  blocking collectives  183 us (36%)
  matrix products  50.8 us (10%)
  other arithmetic  17.1 us (3%)
  between operations  14 us (3%)
  local copies, waits for them, and re-layouts  8.61 us (2%)
    psum x2, waiting for transfers between devices, shards(): updates = lax.psum(update_part, 'ka')  138 us
    all_gather x4, blocking collectives, merged_2(): gathered = jax.tree.map(lambda a: lax.all_gather(a, axis), part)  106 us
    psum x3, waiting for transfers between devices, key_rows(): return lax.psum(contract_rows(weights, updates), 'pb')  92.1 us
    all_gather x2, blocking collectives, residual_total(): return jnp.sum(lax.all_gather(column_part, 'ka'), axis=0)  38.7 us
    psum x2, blocking collectives, direction_total(): return lax.psum(column_part, 'ka')  38.5 us
    dot_general x9, matrix products, contract_cols(): lax.dot_general(left_side, right_side, (((1,), (1,)), ((), ())), precisio...  19.5 us
    dot_general x8, matrix products, shards(): jnp.dot(exponent_block, values_block, precision=highest, preferred_elemen...  17 us
  transfers between devices with their start and end apart: 6, of which 5 were waited for; matrix products, arithmetic and copies ran while one was open for 2% of the time, Pallas kernels for 0%

profile of v1, /device:TPU:0, one launch (start us, length us, event | category | flops | bytes accessed | tf_op | source)
XLA Modules:
  0.0 504.2 jit_solution(15698568379458818211)
XLA Ops:
  7.5 3.1 multiply_reduce_fusion
  10.6 3.0 multiply_reduce_fusion.1
  13.7 2.0 multiply_reduce_fusion.2
  15.6 2.0 multiply_reduce_fusion.3
  17.6 2.0 multiply_reduce_fusion.4
  19.6 2.0 multiply_reduce_fusion.5
  21.6 2.4 multiply_reduce_fusion.6
  24.0 2.0 multiply_reduce_fusion.7
  26.1 2.0 fusion.18
  28.1 2.0 fusion.19
  30.1 2.0 fusion.20
  32.1 2.0 fusion.21
  34.1 2.2 fusion.22
  36.3 2.0 fusion.23
  38.4 2.1 fusion.36
  40.5 2.7 fusion.37
  43.8 1.1 copy-done.2
  50.7 28.0 %all-gather.5 = f32[8,1,512]{2,1,0:T(1,128)S(1)} all-gather(f32[1,1,512]{2,1,0:T(1,128)S(1)} %get-tuple-element.317), channel_id=1, replica_groups=mesh['pb'=4,'ka'=8] {'ka'}, dimensions={0}, use_global_device_ids=true | all-gather | bytes 18432 | tf_op jit(solution)/shard_map/all_gather | solution.py:13
  78.7 26.2 %all-gather.6 = f32[8,1,512]{2,1,0:T(1,128)S(1)} all-gather(f32[1,1,512]{2,1,0:T(1,128)S(1)} %get-tuple-element.316), channel_id=1, replica_groups=mesh['pb'=4,'ka'=8] {'ka'}, dimensions={0}, use_global_device_ids=true | all-gather | bytes 18432 | tf_op jit(solution)/shard_map/all_gather | solution.py:13
  105.0 3.2 gather_fusion
  108.2 1.1 fusion.106
  109.2 26.0 %all-gather.7 = f32[8,1,512]{2,1,0:T(1,128)S(1)} all-gather(f32[1,1,512]{2,1,0:T(1,128)S(1)} %bitcast.76), channel_id=3, replica_groups=mesh['pb'=4,'ka'=8] {'ka'}, dimensions={0}, use_global_device_ids=true | all-gather | bytes 18432 | tf_op jit(solution)/shard_map/all_gather | solution.py:13
  135.5 26.0 %all-gather.8 = f32[8,1,512]{2,1,0:T(1,128)S(1)} all-gather(f32[1,1,512]{2,1,0:T(1,128)S(1)} %bitcast.93), channel_id=4, replica_groups=mesh['pb'=4,'ka'=8] {'ka'}, dimensions={0}, use_global_device_ids=true | all-gather | bytes 18432 | tf_op jit(solution)/shard_map/all_gather | solution.py:13
  162.4 9.3 %while.23 = (s32[]{:T(128)}, f32[512]{0:T(512)S(1)}, f32[512]{0:T(512)S(1)}, f32[512,128]{1,0:T(8,128)S(1)}, f32[512]{0:T(512)S(1)}, /*index=5*/f32[512]{0:T(512...) while((s32[]{:T(128)}, f32[512]{0:T(512)S(1)}, ...), condition=%wide.region_19.20_spmd, body=%wide.region_18.19_spmd.sunk | while | flops 202757 | bytes 835779 | solution.py:18
  162.5 1.2 fusion.120
  163.9 1.2 fusion.120
  165.2 1.2 fusion.120
  166.5 1.2 fusion.120
  167.8 1.2 fusion.120
  169.2 1.2 fusion.120
  170.5 1.2 fusion.120
  171.7 1.8 fusion.88
  173.6 29.4 %all-reduce.6.cloned.1.call-done = f32[512,128]{1,0:T(8,128)} async-done(((f32[512,128]{1,0:T(8,128)}), f32[512,128]{1,0:T(8,128)}) %all-reduce.6.cloned.1.call-update) | async-done | bytes 262160 | tf_op jit(solution)/shard_map/psum | solution.py:67
  203.0 3.5 fusion.86
  206.6 70.7 %all-reduce.8.cloned.1.call-done = f32[512,128]{1,0:T(8,128)} async-done(((f32[512,128]{1,0:T(8,128)}), f32[512,128]{1,0:T(8,128)}) %all-reduce.8.cloned.1.call-update) | async-done | bytes 262160 | tf_op jit(solution)/shard_map/psum | solution.py:136
  277.2 2.7 fusion.84
  280.0 31.4 %all-reduce.10.cloned.1.call-done = f32[512,128]{1,0:T(8,128)} async-done(((f32[512,128]{1,0:T(8,128)}), f32[512,128]{1,0:T(8,128)}) %all-reduce.10.cloned.1.call-update) | async-done | bytes 262160 | tf_op jit(solution)/shard_map/psum | solution.py:67
  311.4 1.0 multiply_reduce_fusion.10
  312.4 20.4 %all-gather.9 = f32[8,1,128]{2,1,0:T(1,128)S(1)} all-gather(f32[1,1,128]{2,1,0:T(1,128)S(1)} %bitcast.102), channel_id=5, replica_groups=mesh['pb'=4,'ka'=8] {'ka'}, dimensions={0}, use_global_device_ids=true | all-gather | bytes 4608 | tf_op jit(solution)/shard_map/all_gather | solution.py:78
  332.8 17.1 %psum.52 = f32[128]{0:T(128)S(1)} all-reduce(f32[128]{0:T(128)S(1)} %get-tuple-element.276), channel_id=1, replica_groups=mesh['pb'=4,'ka'=8] {'ka'}, use_global_device_ids=true, to_apply=%region_26.27 | all-reduce | flops 128 | bytes 1024 | tf_op jit(solution)/shard_map/psum | solution.py:82
  349.9 1.0 multiply_reduce_fusion.9
  351.0 18.3 %all-gather.10 = f32[8,1,128]{2,1,0:T(1,128)S(1)} all-gather(f32[1,1,128]{2,1,0:T(1,128)S(1)} %bitcast.103), channel_id=6, replica_groups=mesh['pb'=4,'ka'=8] {'ka'}, dimensions={0}, use_global_device_ids=true | all-gather | bytes 4608 | tf_op jit(solution)/shard_map/all_gather | solution.py:78
  369.3 3.5 fusion.82
  372.9 66.9 %all-reduce.12.cloned.1.call-done = f32[512,128]{1,0:T(8,128)} async-done(((f32[512,128]{1,0:T(8,128)}), f32[512,128]{1,0:T(8,128)}) %all-reduce.12.cloned.1.call-update) | async-done | bytes 262160 | tf_op jit(solution)/shard_map/psum | solution.py:136
  439.8 2.7 fusion.80
  442.5 31.4 %all-reduce.14.cloned.1.call-done = f32[512,128]{1,0:T(8,128)} async-done(((f32[512,128]{1,0:T(8,128)}), f32[512,128]{1,0:T(8,128)}) %all-reduce.14.cloned.1.call-update) | async-done | bytes 262160 | tf_op jit(solution)/shard_map/psum | solution.py:67
  473.9 1.1 multiply_reduce_fusion.8
  475.0 21.3 %psum.55 = f32[128]{0:T(128)S(1)} all-reduce(f32[128]{0:T(128)S(1)} %multiply_reduce_fusion.8), channel_id=1, replica_groups=mesh['pb'=4,'ka'=8] {'ka'}, use_global_device_ids=true, to_apply=%region_32.33 | all-reduce | flops 128 | bytes 1024 | tf_op jit(solution)/shard_map/psum | solution.py:82
  (117 shorter events, 10.2 us)
Async XLA Ops:
  6.5 1.0 copy-start
  6.5 154.9 %all-gather.13.cloned.1.call-start = ((), (), s32[]{:S(2)}) async-start(), calls=%async_computation.5 | async-start | bytes 2359296 | tf_op jit(solution)/shard_map/all_gather | solution.py:13
  7.5 6.2 %copy-start.15 = (f32[8192,128]{1,0:T(8,128)S(1)}, f32[8192,128]{1,0:T(8,128)}, u32[]{:S(2)}) copy-start(f32[8192,128]{1,0:T(8,128)} %param.7) | copy-start | bytes 12582916
  13.7 12.4 %copy-start.1 = (f32[512,1024]{1,0:T(8,128)}, f32[512,1024]{1,0:T(8,128)S(1)}, u32[]{:S(2)}) copy-start(f32[512,1024]{1,0:T(8,128)S(1)} %get-tuple-element.344) | copy-start | bytes 6291460
  15.6 12.4 %copy-start.3 = (f32[512,1024]{1,0:T(8,128)}, f32[512,1024]{1,0:T(8,128)S(1)}, u32[]{:S(2)}) copy-start(f32[512,1024]{1,0:T(8,128)S(1)} %get-tuple-element.346) | copy-start | bytes 6291460
  17.6 12.5 %copy-start.5 = (f32[512,1024]{1,0:T(8,128)}, f32[512,1024]{1,0:T(8,128)S(1)}, u32[]{:S(2)}) copy-start(f32[512,1024]{1,0:T(8,128)S(1)} %get-tuple-element.348) | copy-start | bytes 6291460
  19.6 12.5 %copy-start.7 = (f32[512,1024]{1,0:T(8,128)}, f32[512,1024]{1,0:T(8,128)S(1)}, u32[]{:S(2)}) copy-start(f32[512,1024]{1,0:T(8,128)S(1)} %get-tuple-element.350) | copy-start | bytes 6291460
  21.6 12.6 %copy-start.9 = (f32[512,1024]{1,0:T(8,128)}, f32[512,1024]{1,0:T(8,128)S(1)}, u32[]{:S(2)}) copy-start(f32[512,1024]{1,0:T(8,128)S(1)} %get-tuple-element.352) | copy-start | bytes 6291460
  21.6 4.5 copy-start.18
  24.0 12.3 %copy-start.11 = (f32[512,1024]{1,0:T(8,128)}, f32[512,1024]{1,0:T(8,128)S(1)}, u32[]{:S(2)}) copy-start(f32[512,1024]{1,0:T(8,128)S(1)} %get-tuple-element.354) | copy-start | bytes 6291460
  26.0 12.4 %copy-start.13 = (f32[512,1024]{1,0:T(8,128)}, f32[512,1024]{1,0:T(8,128)S(1)}, u32[]{:S(2)}) copy-start(f32[512,1024]{1,0:T(8,128)S(1)} %get-tuple-element.356) | copy-start | bytes 6291460
  43.2 159.8 %all-reduce.6.cloned.1.call-start = ((), (), s32[]{:S(2)}) async-start(), calls=%async_computation | async-start | bytes 524288 | tf_op jit(solution)/shard_map/psum | solution.py:67
  43.3 1.6 copy-start.2
  43.3 2.2 copy-start.4
  44.9 1.7 copy-start.6
  45.5 1.7 copy-start.8
  46.6 1.7 copy-start.10
  47.2 1.7 copy-start.12
  48.3 1.7 copy-start.14
  48.9 56.0 %copy-start.19 = (s32[512]{0:T(512)S(1)}, s32[512]{0:T(512)}, u32[]{:S(2)}) copy-start(s32[512]{0:T(512)} %param.9) | copy-start | bytes 6148
  173.6 103.7 %all-reduce.8.cloned.1.call-start = ((), (), s32[]{:S(2)}) async-start(), calls=%async_computation.1 | async-start | bytes 524288 | tf_op jit(solution)/shard_map/psum | solution.py:136
  203.0 108.4 %copy-start.16 = (f32[512,128]{1,0:T(8,128)S(1)}, f32[512,128]{1,0:T(8,128)}, u32[]{:S(2)}) copy-start(f32[512,128]{1,0:T(8,128)} %all-reduce.6.cloned.1.call-done) | copy-start | bytes 786436
  206.5 104.8 %all-reduce.10.cloned.1.call-start = ((), (), s32[]{:S(2)}) async-start(), calls=%async_computation.2 | async-start | bytes 524288 | tf_op jit(solution)/shard_map/psum | solution.py:67
  280.0 159.8 %all-reduce.12.cloned.1.call-start = ((), (), s32[]{:S(2)}) async-start(), calls=%async_computation.3 | async-start | bytes 524288 | tf_op jit(solution)/shard_map/psum | solution.py:136
  351.0 123.0 %copy-start.17 = (f32[512,128]{1,0:T(8,128)S(1)}, f32[512,128]{1,0:T(8,128)}, u32[]{:S(2)}) copy-start(f32[512,128]{1,0:T(8,128)} %all-reduce.10.cloned.1.call-done) | copy-start | bytes 786436
  372.9 101.1 %all-reduce.14.cloned.1.call-start = ((), (), s32[]{:S(2)}) async-start(), calls=%async_computation.4 | async-start | bytes 524288 | tf_op jit(solution)/shard_map/psum | solution.py:67
Sparse Core Ops, SparseCore 0:
  43.3 52.1 all-gather.12
  173.7 29.2 all-reduce.5
  206.7 70.5 all-reduce.7
  280.1 31.2 all-reduce.9
  373.0 66.7 all-reduce.11
  442.6 31.2 all-reduce.13
